TPU v7x, 32 devices: a whole 2x2x4 slice. The times are simulated.
32 devices in a mesh: groups: 2 (over y), row: 4 (over z), col: 4 (over x, core).
Axes of the slice: x: 2, y: 2, z: 4, core: 2. Of those that a mesh axis runs over, the one named last changes fastest.
Arguments:
- queries: bfloat16 [4096, 1024], P(('groups', 'row'), 'col'), parts along dimension 0, may hold values from -64 to 64
- keys: bfloat16 [4096, 1024], P(('groups', 'col'), 'row'), parts along dimension 0, may hold values from -6 to 6
- values: bfloat16 [4096, 1024], P(('groups', 'col'), 'row'), parts along dimension 0, may hold values from -6 to 6
- cotangent: bfloat16 [4096, 1024], P(('groups', 'row'), 'col'), parts along dimension 0, may hold values from -6 to 6
- block_lists: int32 [32, 16], P(('groups', 'row')), parts along dimension 0, may hold values from 0 to 15, as said below
- block_counts: int32 [32], P(('groups', 'row')), parts along dimension 0, may hold values from 1 to 16, as said below
Outputs:
- attended: bfloat16 [4096, 1024], P(('groups', 'row'), 'col'), parts along dimension 0
- grad_queries: bfloat16 [4096, 1024], P(('groups', 'row'), 'col'), parts along dimension 0
- grad_keys: bfloat16 [4096, 1024], P(('groups', 'col'), 'row'), parts along dimension 0
- grad_values: bfloat16 [4096, 1024], P(('groups', 'col'), 'row'), parts along dimension 0
There are 2 independent parts, one for each index of `groups`. A program takes and returns all parts, laid end to end along the dimension named above; each array names one. Nothing has to cross between parts.
Inputs may be any that keep to these rules, and one draw needn't show every extreme that they name: `block_lists`: each row lists 16 distinct blocks; its first entry is the query block itself. `block_counts`: some query block has all 16 entries live in every draw.
All inputs are finite; a program needn't handle non-finite values.
Results may differ from a plain program's by a relative error of at most 0.011.
Values may be sent and summed in bfloat16 or wider, within the bound.
No kernel may reach another device: no remote copies, remote signals or barrier semaphores. Data moves between devices by JAX's collectives and lax.ppermute only.
A program may use at most 64 MiB of HBM per device.

v0:
```python
import math
import jax
import jax.numpy as jnp
from jax import lax
from jax.sharding import PartitionSpec as P

D = 1024
HEADS = 16
HEAD = 64
BLK = 128
MAXNB = 16
NEG_FILL = -1e30


def tile_scores(query_tile, key_tile, score_scale):
    query_heads = query_tile.reshape(query_tile.shape[0], HEADS, -1)
    key_heads = key_tile.reshape(key_tile.shape[0], HEADS, -1)
    return (
        jnp.einsum("qhd,khd->hqk", query_heads, key_heads, preferred_element_type=jnp.float32)
        * score_scale
    )


def on_device(queries, keys, values, cotangent, block_lists, block_counts):
    score_scale = 1.0 / math.sqrt(HEAD)
    q_full = lax.all_gather(queries, "col", axis=1, tiled=True)
    k_full, v_full = (
        lax.all_gather(keys, "row", axis=1, tiled=True),
        lax.all_gather(values, "row", axis=1, tiled=True),
    )
    q_rows = q_full.shape[0]
    k_rows = k_full.shape[0]
    q_blocks = q_rows // BLK
    k_blocks = k_rows // BLK
    group_size = min(4, q_blocks)
    span_rows = group_size * BLK
    supers = q_blocks // group_size
    tile_count = supers * k_blocks
    first_key = lax.axis_index("col") * k_blocks
    wanted = first_key + jnp.arange(k_blocks, dtype=jnp.int32)
    live_slots = jnp.arange(MAXNB, dtype=jnp.int32)[None, :] < block_counts[:, None]
    block_hit = jnp.any(
        (block_lists[:, :, None] == wanted[None, None, :]) & live_slots[:, :, None], axis=1
    )
    block_hit = block_hit.reshape(supers, group_size, k_blocks).transpose(0, 2, 1)
    row_mask = jnp.repeat(block_hit, BLK, axis=2)
    tile_any = jnp.any(block_hit, axis=2)

    def tile_parts(step):
        super_at = step // k_blocks
        key_at = step % k_blocks
        query_tile = lax.dynamic_slice_in_dim(q_full, super_at * span_rows, span_rows, 0)
        key_tile = lax.dynamic_slice_in_dim(k_full, key_at * BLK, BLK, 0)
        value_tile = lax.dynamic_slice_in_dim(v_full, key_at * BLK, BLK, 0)
        keep_mask = row_mask[super_at, key_at][None, :, None]
        return (super_at, key_at, query_tile, key_tile, value_tile, keep_mask)

    def unchanged(carry):
        return carry

    def stats_step(step, carry):
        super_at, key_at, query_tile, key_tile, value_tile, keep_mask = tile_parts(step)

        def stats_work(state):
            row_top, row_total = state
            scores = jnp.where(keep_mask, tile_scores(query_tile, key_tile, score_scale), NEG_FILL)
            old_top = lax.dynamic_slice_in_dim(row_top, super_at * span_rows, span_rows, 1)
            old_total = lax.dynamic_slice_in_dim(row_total, super_at * span_rows, span_rows, 1)
            new_top = jnp.maximum(old_top, jnp.max(scores, axis=2))
            exp_terms = jnp.where(keep_mask, jnp.exp(scores - new_top[:, :, None]), 0.0)
            fresh = old_total * jnp.exp(old_top - new_top) + jnp.sum(exp_terms, axis=2)
            return (
                lax.dynamic_update_slice_in_dim(row_top, new_top, super_at * span_rows, 1),
                lax.dynamic_update_slice_in_dim(row_total, fresh, super_at * span_rows, 1),
            )

        return lax.cond(tile_any[super_at, key_at], stats_work, unchanged, carry)

    start_top = jnp.full((HEADS, q_rows), NEG_FILL, jnp.float32)
    start_total = jnp.zeros((HEADS, q_rows), jnp.float32)
    local_top, local_total = lax.fori_loop(0, tile_count, stats_step, (start_top, start_total))
    row_top = lax.pmax(local_top.astype(jnp.bfloat16), "col").astype(local_top.dtype)
    row_total = lax.psum(local_total * jnp.exp(local_top - row_top), "col")

    def tile_weights(scores, super_at, keep_mask):
        top_rows = lax.dynamic_slice_in_dim(row_top, super_at * span_rows, span_rows, 1)
        total_rows = lax.dynamic_slice_in_dim(row_total, super_at * span_rows, span_rows, 1)
        ratio = jnp.exp(scores - top_rows[:, :, None]) / total_rows[:, :, None]
        return jnp.where(keep_mask, ratio, 0.0).astype(jnp.bfloat16)

    def output_step(step, carry):
        super_at, key_at, query_tile, key_tile, value_tile, keep_mask = tile_parts(step)

        def output_work(out_rows):
            scores = jnp.where(keep_mask, tile_scores(query_tile, key_tile, score_scale), NEG_FILL)
            weights = tile_weights(scores, super_at, keep_mask)
            value_heads = value_tile.reshape(BLK, HEADS, -1)
            part = jnp.einsum(
                "hqk,khd->qhd", weights, value_heads, preferred_element_type=jnp.float32
            ).reshape(span_rows, -1)
            current = lax.dynamic_slice_in_dim(out_rows, super_at * span_rows, span_rows, 0)
            return lax.dynamic_update_slice_in_dim(
                out_rows, current + part, super_at * span_rows, 0
            )

        return lax.cond(tile_any[super_at, key_at], output_work, unchanged, carry)

    partial_out = lax.fori_loop(0, tile_count, output_step, jnp.zeros((q_rows, D), jnp.float32))
    out_share = lax.psum_scatter(partial_out, "col", scatter_dimension=1, tiled=True).astype(
        jnp.bfloat16
    )
    grad_full, out_full = (
        lax.all_gather(cotangent, "col", axis=1, tiled=True),
        lax.all_gather(out_share, "col", axis=1, tiled=True),
    )
    delta = jnp.einsum(
        "qhd,qhd->hq",
        grad_full.reshape(q_rows, HEADS, -1),
        out_full.reshape(q_rows, HEADS, -1),
        preferred_element_type=jnp.float32,
    )

    def grad_step(step, carry):
        super_at, key_at, query_tile, key_tile, value_tile, keep_mask = tile_parts(step)

        def grad_work(state):
            query_accum, key_accum, value_accum = state
            scores = jnp.where(keep_mask, tile_scores(query_tile, key_tile, score_scale), NEG_FILL)
            weights = tile_weights(scores, super_at, keep_mask)
            grad_tile = lax.dynamic_slice_in_dim(
                grad_full, super_at * span_rows, span_rows, 0
            ).reshape(span_rows, HEADS, -1)
            value_heads = value_tile.reshape(BLK, HEADS, -1)
            key_heads = key_tile.reshape(BLK, HEADS, -1)
            query_heads = query_tile.reshape(span_rows, HEADS, -1)
            dweights = jnp.einsum(
                "qhd,khd->hqk", grad_tile, value_heads, preferred_element_type=jnp.float32
            )
            delta_rows = lax.dynamic_slice_in_dim(delta, super_at * span_rows, span_rows, 1)
            dscores = (weights.astype(jnp.float32) * (dweights - delta_rows[:, :, None])).astype(
                jnp.bfloat16
            )
            query_part = score_scale * jnp.einsum(
                "hqk,khd->qhd", dscores, key_heads, preferred_element_type=jnp.float32
            )
            key_part = score_scale * jnp.einsum(
                "hqk,qhd->khd", dscores, query_heads, preferred_element_type=jnp.float32
            )
            value_part = jnp.einsum(
                "hqk,qhd->khd", weights, grad_tile, preferred_element_type=jnp.float32
            )
            query_now = lax.dynamic_slice_in_dim(query_accum, super_at * span_rows, span_rows, 0)
            key_now = lax.dynamic_slice_in_dim(key_accum, key_at * BLK, BLK, 0)
            value_now = lax.dynamic_slice_in_dim(value_accum, key_at * BLK, BLK, 0)
            query_accum = lax.dynamic_update_slice_in_dim(
                query_accum, query_now + query_part.reshape(span_rows, -1), super_at * span_rows, 0
            )
            key_accum = lax.dynamic_update_slice_in_dim(
                key_accum, key_now + key_part.reshape(BLK, -1), key_at * BLK, 0
            )
            value_accum = lax.dynamic_update_slice_in_dim(
                value_accum, value_now + value_part.reshape(BLK, -1), key_at * BLK, 0
            )
            return (query_accum, key_accum, value_accum)

        return lax.cond(tile_any[super_at, key_at], grad_work, unchanged, carry)

    start_grads = (
        jnp.zeros((q_rows, D), jnp.float32),
        jnp.zeros((k_rows, D), jnp.float32),
        jnp.zeros((k_rows, D), jnp.float32),
    )
    query_parts, key_parts, value_parts = lax.fori_loop(0, tile_count, grad_step, start_grads)
    grad_queries = lax.psum_scatter(query_parts, "col", scatter_dimension=1, tiled=True).astype(
        jnp.bfloat16
    )
    grad_keys, grad_values = (
        lax.psum_scatter(key_parts, "row", scatter_dimension=1, tiled=True),
        lax.psum_scatter(value_parts, "row", scatter_dimension=1, tiled=True),
    )
    return (
        out_share,
        grad_queries,
        grad_keys.astype(jnp.bfloat16),
        grad_values.astype(jnp.bfloat16),
    )


def solution(mesh):
    return jax.shard_map(
        on_device,
        mesh=mesh,
        in_specs=(
            P(("groups", "row"), "col"),
            P(("groups", "col"), "row"),
            P(("groups", "col"), "row"),
            P(("groups", "row"), "col"),
            P(("groups", "row"), None),
            P(("groups", "row")),
        ),
        out_specs=(
            P(("groups", "row"), "col"),
            P(("groups", "row"), "col"),
            P(("groups", "col"), "row"),
            P(("groups", "col"), "row"),
        ),
        check_vma=False,
    )
```

profile of v0, /device:TPU:0, one launch (start us, length us, event | category | flops | bytes accessed | tf_op | source)
XLA Modules:
  0.0 402.9 jit_solution(14908098541145584658)
XLA Ops:
  13.3 16.3 %all-gather.8.cloned.1.call-done = bf16[512,1024]{0,1:T(8,128)(2,1)} async-done(((bf16[512,256]{0,1:T(8,128)(2,1)}), bf16[512,1024]{0,1:T(8,128)(2,1)}) %all-gather.8.cloned.1.call-update) | async-done | bytes 1048592 | tf_op jit(solution)/shard_map/all_gather | solution.py:26
  29.6 30.1 %all-gather.6.cloned.1.call-done = bf16[512,1024]{0,1:T(8,128)(2,1)} async-done(((bf16[512,256]{0,1:T(8,128)(2,1)}), bf16[512,1024]{0,1:T(8,128)(2,1)}) %all-gather.6.cloned.1.call-update) | async-done | bytes 1048592 | tf_op jit(solution)/shard_map/all_gather | solution.py:28
  59.7 21.9 %while.57 = (s32[]{:T(128)}, f32[16,512]{1,0:T(8,128)S(1)}, f32[16,512]{1,0:T(8,128)S(1)}, pred[1,4]{1,0:T(4,128)(4,1)S(1)}, bf16[512,1024]{0,1:T(8,128)(2,1)}, ...) while((s32[]{:T(128)}, f32[16,512]{1,0:T(8,128)S(1)}, ...), condition=%wide.region_7.8_spmd.clone, body=%wide.region_2.7_spmd.clone.sunk | while | flops 142622736 | bytes 10658168 | solution.py:81
  65.8 4.9 %conditional.9 = ((f32[16,512]{1,0:T(8,128)S(1)}, f32[16,512]{1,0:T(8,128)S(1)})) conditional(s32[]{:T(128)} %bitcast.68, (f32[16,512]{1,0:T(8,128)S(1)}, f32[16,512]{1,0:T(8,128)S(1)}) %tuple.194, (pred[4,4]{1,0:T(4,128)(4,1)S(1)}, s32[]{:T(128)}, s32[]{:T(128)}, bf16[512,1024]{0,1:T(8,128)(2,1)}, bf16[512,1024]{0,1:T(8,128)(2,1)}, ...), branch_computations={%region_3.3_spmd, %region_4.6_spmd} | conditional | flops 142622720 | bytes 10657886 | solution.py:77
  71.3 4.8 %conditional.9 = ((f32[16,512]{1,0:T(8,128)S(1)}, f32[16,512]{1,0:T(8,128)S(1)})) conditional(s32[]{:T(128)} %bitcast.68, (f32[16,512]{1,0:T(8,128)S(1)}, f32[16,512]{1,0:T(8,128)S(1)}) %tuple.194, (pred[4,4]{1,0:T(4,128)(4,1)S(1)}, s32[]{:T(128)}, s32[]{:T(128)}, bf16[512,1024]{0,1:T(8,128)(2,1)}, bf16[512,1024]{0,1:T(8,128)(2,1)}, ...), branch_computations={%region_3.3_spmd, %region_4.6_spmd} | conditional | flops 142622720 | bytes 10657886 | solution.py:77
  76.8 4.8 %conditional.9 = ((f32[16,512]{1,0:T(8,128)S(1)}, f32[16,512]{1,0:T(8,128)S(1)})) conditional(s32[]{:T(128)} %bitcast.68, (f32[16,512]{1,0:T(8,128)S(1)}, f32[16,512]{1,0:T(8,128)S(1)}) %tuple.194, (pred[4,4]{1,0:T(4,128)(4,1)S(1)}, s32[]{:T(128)}, s32[]{:T(128)}, bf16[512,1024]{0,1:T(8,128)(2,1)}, bf16[512,1024]{0,1:T(8,128)(2,1)}, ...), branch_computations={%region_3.3_spmd, %region_4.6_spmd} | conditional | flops 142622720 | bytes 10657886 | solution.py:77
  81.6 11.3 %pmax.7 = bf16[16,512]{1,0:T(8,128)(2,1)S(1)} all-reduce(bf16[16,512]{1,0:T(8,128)(2,1)S(1)} %convert_element_type.89), channel_id=1, replica_groups=mesh['groups'=2,'row'=4,'col'=4] {'col'}, use_global_device_ids=true, to_apply=%region_8.9 | all-reduce | flops 8192 | bytes 32768 | tf_op jit(solution)/shard_map/pmax | solution.py:82
  92.9 10.3 %psum.7 = f32[16,512]{1,0:T(8,128)S(1)} all-reduce(f32[16,512]{1,0:T(8,128)S(1)} %exponential_multiply_fusion), channel_id=1, replica_groups=mesh['groups'=2,'row'=4,'col'=4] {'col'}, use_global_device_ids=true, to_apply=%region_9.10 | all-reduce | flops 8192 | bytes 65536 | tf_op jit(solution)/shard_map/psum | solution.py:83
  103.5 36.9 %while.58 = (s32[]{:T(128)}, f32[512,1024]{0,1:T(8,128)S(1)}, pred[1,4]{1,0:T(4,128)(4,1)S(1)}, bf16[512,1024]{0,1:T(8,128)(2,1)}, bf16[512,1024]{0,1:T(8,128)(2...) while((s32[]{:T(128)}, f32[512,1024]{0,1:T(8,128)S(1)}, ...), condition=%wide.region_13.14_spmd.clone, body=%wide.region_10.13_spmd.clone.sunk | while | flops 275251200 | bytes 11083640 | solution.py:108
  104.2 8.6 %conditional.10 = (f32[512,1024]{0,1:T(8,128)S(1)}) conditional(s32[]{:T(128)} %bitcast.69, f32[512,1024]{0,1:T(8,128)S(1)} %get-tuple-element.1617, (pred[4,4]{1,0:T(4,128)(4,1)S(1)}, s32[]{:T(128)}, s32[]{:T(128)}, bf16[512,1024]{0,1:T(8,128)(2,1)}, bf16[512,1024]{0,1:T(8,128)(2,1)S(1)}, /*index=5*/f32[16,512]{1,0:T(8,128)S(1)}, ...), branch_computations={%region_11.11_spmd, %region_12.12_spmd} | conditional | flops 275251200 | bytes 11083342 | solution.py:106
  113.4 8.6 %conditional.10 = (f32[512,1024]{0,1:T(8,128)S(1)}) conditional(s32[]{:T(128)} %bitcast.69, f32[512,1024]{0,1:T(8,128)S(1)} %get-tuple-element.1617, (pred[4,4]{1,0:T(4,128)(4,1)S(1)}, s32[]{:T(128)}, s32[]{:T(128)}, bf16[512,1024]{0,1:T(8,128)(2,1)}, bf16[512,1024]{0,1:T(8,128)(2,1)S(1)}, /*index=5*/f32[16,512]{1,0:T(8,128)S(1)}, ...), branch_computations={%region_11.11_spmd, %region_12.12_spmd} | conditional | flops 275251200 | bytes 11083342 | solution.py:106
  122.6 8.6 %conditional.10 = (f32[512,1024]{0,1:T(8,128)S(1)}) conditional(s32[]{:T(128)} %bitcast.69, f32[512,1024]{0,1:T(8,128)S(1)} %get-tuple-element.1617, (pred[4,4]{1,0:T(4,128)(4,1)S(1)}, s32[]{:T(128)}, s32[]{:T(128)}, bf16[512,1024]{0,1:T(8,128)(2,1)}, bf16[512,1024]{0,1:T(8,128)(2,1)S(1)}, /*index=5*/f32[16,512]{1,0:T(8,128)S(1)}, ...), branch_computations={%region_11.11_spmd, %region_12.12_spmd} | conditional | flops 275251200 | bytes 11083342 | solution.py:106
  131.9 8.6 %conditional.10 = (f32[512,1024]{0,1:T(8,128)S(1)}) conditional(s32[]{:T(128)} %bitcast.69, f32[512,1024]{0,1:T(8,128)S(1)} %get-tuple-element.1617, (pred[4,4]{1,0:T(4,128)(4,1)S(1)}, s32[]{:T(128)}, s32[]{:T(128)}, bf16[512,1024]{0,1:T(8,128)(2,1)}, bf16[512,1024]{0,1:T(8,128)(2,1)S(1)}, /*index=5*/f32[16,512]{1,0:T(8,128)S(1)}, ...), branch_computations={%region_11.11_spmd, %region_12.12_spmd} | conditional | flops 275251200 | bytes 11083342 | solution.py:106
  142.8 29.6 %reduce-scatter.5.cloned.1.call-done = f32[512,256]{0,1:T(8,128)} async-done(((f32[512,1024]{0,1:T(8,128)}), f32[512,256]{0,1:T(8,128)}) %reduce-scatter.5.cloned.1.call-update) | async-done | bytes 524304 | tf_op jit(solution)/shard_map/reduce_scatter | solution.py:109
  174.2 17.0 %all-gather.12.cloned.1.call-done = bf16[512,1024]{0,1:T(8,128)(2,1)} async-done(((bf16[512,256]{0,1:T(8,128)(2,1)}), bf16[512,1024]{0,1:T(8,128)(2,1)}) %all-gather.12.cloned.1.call-update) | async-done | bytes 1048592 | tf_op jit(solution)/shard_map/all_gather | solution.py:113
  191.2 18.8 %all-gather.14.cloned.1.call-done = bf16[512,1024]{0,1:T(8,128)(2,1)} async-done(((bf16[512,256]{0,1:T(8,128)(2,1)}), bf16[512,1024]{0,1:T(8,128)(2,1)}) %all-gather.14.cloned.1.call-update) | async-done | bytes 1048592 | tf_op jit(solution)/shard_map/all_gather | solution.py:114
  216.6 51.4 %while.59 = (s32[]{:T(128)}, f32[512,1024]{0,1:T(8,128)}, f32[512,1024]{0,1:T(8,128)}, f32[512,1024]{0,1:T(8,128)}, pred[1,4]{1,0:T(4,128)(4,1)S(1)}, /*index=5*...) while((s32[]{:T(128)}, f32[512,1024]{0,1:T(8,128)}, ...), condition=%wide.region_18.19_spmd.clone, body=%wide.region_15.18_spmd.clone.sunk | while | flops 683016192 | bytes 48078884 | solution.py:173
  217.2 12.3 %conditional.11 = ((f32[512,1024]{0,1:T(8,128)}, f32[512,1024]{0,1:T(8,128)}, f32[512,1024]{0,1:T(8,128)})) conditional(s32[]{:T(128)} %bitcast.70, (f32[512,1024]{0,1:T(8,128)}, f32[512,1024]{0,1:T(8,128)}, f32[512,1024]{0,1:T(8,128)}) %tuple.199, (pred[4,4]{1,0:T(4,128)(4,1)S(1)}, s32[]{:T(128)}, s32[]{:T(128)}, bf16[512,1024]{0,1:T(8,128)(2,1)}, ...), branch_computations={%region_16.16_spmd, %region_17.17_spmd} | conditional | flops 683016192 | bytes 48078500 | solution.py:166
  230.1 12.3 %conditional.11 = ((f32[512,1024]{0,1:T(8,128)}, f32[512,1024]{0,1:T(8,128)}, f32[512,1024]{0,1:T(8,128)})) conditional(s32[]{:T(128)} %bitcast.70, (f32[512,1024]{0,1:T(8,128)}, f32[512,1024]{0,1:T(8,128)}, f32[512,1024]{0,1:T(8,128)}) %tuple.199, (pred[4,4]{1,0:T(4,128)(4,1)S(1)}, s32[]{:T(128)}, s32[]{:T(128)}, bf16[512,1024]{0,1:T(8,128)(2,1)}, ...), branch_computations={%region_16.16_spmd, %region_17.17_spmd} | conditional | flops 683016192 | bytes 48078500 | solution.py:166
  242.9 12.3 %conditional.11 = ((f32[512,1024]{0,1:T(8,128)}, f32[512,1024]{0,1:T(8,128)}, f32[512,1024]{0,1:T(8,128)})) conditional(s32[]{:T(128)} %bitcast.70, (f32[512,1024]{0,1:T(8,128)}, f32[512,1024]{0,1:T(8,128)}, f32[512,1024]{0,1:T(8,128)}) %tuple.199, (pred[4,4]{1,0:T(4,128)(4,1)S(1)}, s32[]{:T(128)}, s32[]{:T(128)}, bf16[512,1024]{0,1:T(8,128)(2,1)}, ...), branch_computations={%region_16.16_spmd, %region_17.17_spmd} | conditional | flops 683016192 | bytes 48078500 | solution.py:166
  255.8 12.3 %conditional.11 = ((f32[512,1024]{0,1:T(8,128)}, f32[512,1024]{0,1:T(8,128)}, f32[512,1024]{0,1:T(8,128)})) conditional(s32[]{:T(128)} %bitcast.70, (f32[512,1024]{0,1:T(8,128)}, f32[512,1024]{0,1:T(8,128)}, f32[512,1024]{0,1:T(8,128)}) %tuple.199, (pred[4,4]{1,0:T(4,128)(4,1)S(1)}, s32[]{:T(128)}, s32[]{:T(128)}, bf16[512,1024]{0,1:T(8,128)(2,1)}, ...), branch_computations={%region_16.16_spmd, %region_17.17_spmd} | conditional | flops 683016192 | bytes 48078500 | solution.py:166
  279.6 35.4 %reduce-scatter.11.cloned.1.call-done = f32[512,256]{1,0:T(8,128)} async-done(((f32[512,1024]{1,0:T(8,128)}), f32[512,256]{1,0:T(8,128)}) %reduce-scatter.11.cloned.1.call-update) | async-done | bytes 524304 | tf_op jit(solution)/shard_map/reduce_scatter | solution.py:179
  316.8 31.5 %reduce-scatter.7.cloned.1.call-done = f32[512,256]{1,0:T(8,128)} async-done(((f32[512,1024]{1,0:T(8,128)}), f32[512,256]{1,0:T(8,128)}) %reduce-scatter.7.cloned.1.call-update) | async-done | bytes 524304 | tf_op jit(solution)/shard_map/reduce_scatter | solution.py:174
  350.1 44.5 %reduce-scatter.9.cloned.1.call-done = f32[512,256]{1,0:T(8,128)} async-done(((f32[512,1024]{1,0:T(8,128)}), f32[512,256]{1,0:T(8,128)}) %reduce-scatter.9.cloned.1.call-update) | async-done | bytes 524304 | tf_op jit(solution)/shard_map/reduce_scatter | solution.py:178
  (200 shorter events, 140.7 us)
Async XLA Ops:
  7.2 5.7 %copy-start.10 = (s32[4]{0:T(128)S(1)}, s32[4]{0:T(128)}, u32[]{:S(2)}) copy-start(s32[4]{0:T(128)} %param.23) | copy-start | bytes 52
  7.2 5.8 %copy-start.9 = (s32[4,16]{1,0:T(4,128)S(1)}, s32[4,16]{1,0:T(4,128)}, u32[]{:S(2)}) copy-start(s32[4,16]{1,0:T(4,128)} %param.22) | copy-start | bytes 772
  7.2 22.4 %all-gather.8.cloned.1.call-start = ((), (), s32[]{:S(2)}) async-start(), calls=%async_computation.5 | async-start | bytes 1310720 | tf_op jit(solution)/shard_map/all_gather | solution.py:26
  9.1 50.7 %all-gather.6.cloned.1.call-start = ((), (), s32[]{:S(2)}) async-start(), calls=%async_computation.4 | async-start | bytes 1310720 | tf_op jit(solution)/shard_map/all_gather | solution.py:28
  10.9 92.3 %all-gather.10.cloned.1.call-start = ((), (), s32[]{:S(2)}) async-start(), calls=%async_computation.6 | async-start | bytes 1310720 | tf_op jit(solution)/shard_map/all_gather | solution.py:29
  12.8 159.5 %reduce-scatter.5.cloned.1.call-start = ((), (), s32[]{:S(2)}) async-start(), calls=%async_computation.7 | async-start | bytes 2621440 | tf_op jit(solution)/shard_map/reduce_scatter | solution.py:109
  81.6 21.9 %copy-start.1 = (bf16[512,1024]{0,1:T(8,128)(2,1)S(1)}, bf16[512,1024]{0,1:T(8,128)(2,1)}, u32[]{:S(2)}) copy-start(bf16[512,1024]{0,1:T(8,128)(2,1)} %get-tuple-element.1707) | copy-start | bytes 3145732
  140.4 1.4 copy-start.8
  141.8 49.4 %all-gather.12.cloned.1.call-start = ((), (), s32[]{:S(2)}) async-start(), calls=%async_computation.8 | async-start | bytes 1310720 | tf_op jit(solution)/shard_map/all_gather | solution.py:113
  142.7 67.3 %all-gather.14.cloned.1.call-start = ((), (), s32[]{:S(2)}) async-start(), calls=%async_computation.9 | async-start | bytes 1310720 | tf_op jit(solution)/shard_map/all_gather | solution.py:114
  174.1 140.9 %reduce-scatter.11.cloned.1.call-start = ((), (), s32[]{:S(2)}) async-start(), calls=%async_computation.12 | async-start | bytes 2621440 | tf_op jit(solution)/shard_map/reduce_scatter | solution.py:179
  213.5 3.2 copy-start
  223.7 1.6 copy-start.2
  225.8 1.3 copy-start.3
  236.5 1.6 copy-start.2
  238.7 1.3 copy-start.3
  249.4 1.6 copy-start.2
  251.5 1.3 copy-start.3
  262.2 1.6 copy-start.2
  264.4 1.3 copy-start.3
  271.0 1.6 copy-start.4
  271.0 77.3 %reduce-scatter.7.cloned.1.call-start = ((), (), s32[]{:S(2)}) async-start(), calls=%async_computation.10 | async-start | bytes 2621440 | tf_op jit(solution)/shard_map/reduce_scatter | solution.py:174
  274.4 1.6 copy-start.6
  274.4 120.2 %reduce-scatter.9.cloned.1.call-start = ((), (), s32[]{:S(2)}) async-start(), calls=%async_computation.11 | async-start | bytes 2621440 | tf_op jit(solution)/shard_map/reduce_scatter | solution.py:178
  (2 other events, 2.3 us)
Sparse Core Ops, SparseCore 0:
  10.2 19.4 all-gather.7
  31.7 27.9 all-gather.5
  61.9 27.4 all-gather.9
  141.9 30.3 reduce-scatter.4
  174.4 16.7 all-gather.11
  193.2 16.7 all-gather.13
  271.1 43.8 reduce-scatter.10
  317.6 30.7 reduce-scatter.6
  350.7 43.8 reduce-scatter.8
where the time goes:
time: 405 us; the launch traced here: 403 us
  waiting for transfers between devices  223 us (55%)
  local copies, waits for them, and re-layouts  54.1 us (13%)
  other arithmetic  41 us (10%)
  matrix products  40.2 us (10%)
  blocking collectives  21.5 us (5%)
  between operations  14 us (3%)
  loops' own time  8.27 us (2%)
    reduce_scatter x1, waiting for transfers between devices, on_device(): lax.psum_scatter(key_parts, 'row', scatter_dimension=1, tiled=True)  44.5 us
    reduce_scatter x1, waiting for transfers between devices, on_device(): lax.psum_scatter(value_parts, 'row', scatter_dimension=1, tiled=True)  35.4 us
    reduce_scatter x1, waiting for transfers between devices, on_device(): lax.psum_scatter(query_parts, 'col', scatter_dimension=1, tiled=True)  31.5 us
    all_gather x1, waiting for transfers between devices, on_device(): lax.all_gather(keys, 'row', axis=1, tiled=True)  30.1 us
    reduce_scatter x1, waiting for transfers between devices, on_device(): lax.psum_scatter(partial_out, 'col', scatter_dimension=1, tiled=True)  29.6 us
    all_gather x1, waiting for transfers between devices, on_device(): lax.all_gather(out_share, 'col', axis=1, tiled=True)  18.8 us
    all_gather x1, waiting for transfers between devices, on_device(): lax.all_gather(cotangent, 'col', axis=1, tiled=True)  17 us
    all_gather x1, waiting for transfers between devices, on_device(): q_full = lax.all_gather(queries, 'col', axis=1, tiled=True)  16.3 us
  transfers between devices with their start and end apart: 9, of which 8 were waited for; matrix products, arithmetic and copies ran while one was open for 8% of the time, Pallas kernels for 0%

commit v1 on v0

--- a/solution.py
+++ b/solution.py
@@ -23,7 +23,14 @@
 
 def on_device(queries, keys, values, cotangent, block_lists, block_counts):
     score_scale = 1.0 / math.sqrt(HEAD)
-    q_full = lax.all_gather(queries, "col", axis=1, tiled=True)
+    size = lax.axis_size("col")
+    forward = [(i, (i + 1) % size) for i in range(size)]
+    parts = [queries]
+    for stride in range(1, size):
+        parts = [lax.ppermute(parts[0], "col", forward), *parts]
+    whole = jnp.concatenate(parts, axis=1)
+    places = (lax.axis_index("col") + 1) * parts[-1].shape[1]
+    q_full = jnp.roll(whole, places, axis=1)
     k_full, v_full = (
         lax.all_gather(keys, "row", axis=1, tiled=True),
         lax.all_gather(values, "row", axis=1, tiled=True),

time: 405 us -> 382 us (0.943)
  waiting for transfers between devices: 223 us -> 205 us
  matrix products: 40.2 us -> 35.3 us
    all_gather x1, waiting for transfers between devices: 30.1 us -> 12.2 us  [on_device(): lax.all_gather(keys, 'row', axis=1, tiled=True)]
    all_gather x1 -> x0, waiting for transfers between devices: 16.3 us -> none  [on_device(): q_full = lax.all_gather(queries, 'col', axis=1, tiled=True)]
    ppermute x0 -> x3, waiting for transfers between devices: none -> 15.3 us  [on_device(): parts = [lax.ppermute(parts[0], 'col', forward), *parts]]
    dot_general x8, matrix products: 13.5 us -> 8.57 us  [tile_scores(): jnp.einsum('qhd,khd->hqk', query_heads, key_heads, preferred_element_type...]
    unnamed x23 -> x28, local copies, waits for them, and re-layouts: 12.4 us -> 11.8 us
  transfers between devices with their start and end apart: 9 -> 11, of which waited for: 8 -> 10; matrix products, arithmetic and copies ran while one was open for 8% -> 7% of each run, Pallas kernels for 0% -> 0%
where the time goes in v1:
time: 382 us; the launch traced here: 381 us
  waiting for transfers between devices  205 us (54%)
  local copies, waits for them, and re-layouts  53.7 us (14%)
  other arithmetic  41.3 us (11%)
  matrix products  35.3 us (9%)
  blocking collectives  21.8 us (6%)
  between operations  14.3 us (4%)
  loops' own time  8.63 us (2%)
    reduce_scatter x1, waiting for transfers between devices, on_device(): lax.psum_scatter(key_parts, 'row', scatter_dimension=1, tiled=True)  44.5 us
    reduce_scatter x1, waiting for transfers between devices, on_device(): lax.psum_scatter(value_parts, 'row', scatter_dimension=1, tiled=True)  35.4 us
    reduce_scatter x1, waiting for transfers between devices, on_device(): lax.psum_scatter(query_parts, 'col', scatter_dimension=1, tiled=True)  31.5 us
    reduce_scatter x1, waiting for transfers between devices, on_device(): lax.psum_scatter(partial_out, 'col', scatter_dimension=1, tiled=True)  29.6 us
    all_gather x1, waiting for transfers between devices, on_device(): lax.all_gather(out_share, 'col', axis=1, tiled=True)  18.8 us
    all_gather x1, waiting for transfers between devices, on_device(): lax.all_gather(cotangent, 'col', axis=1, tiled=True)  17 us
    dot_general x4, matrix products, output_work(): jnp.einsum('hqk,khd->qhd', weights, value_heads, preferred_element_type=j...  15.3 us
    ppermute x3, waiting for transfers between devices, on_device(): parts = [lax.ppermute(parts[0], 'col', forward), *parts]  15.3 us
  transfers between devices with their start and end apart: 11, of which 10 were waited for; matrix products, arithmetic and copies ran while one was open for 7% of the time, Pallas kernels for 0%

profile of v1, /device:TPU:0, one launch (start us, length us, event | category | flops | bytes accessed | tf_op | source)
XLA Modules:
  0.0 380.5 jit_solution(15680987374808511942)
XLA Ops:
  10.7 6.0 %collective-permute-done = bf16[512,256]{0,1:T(8,128)(2,1)S(1)} collective-permute-done((bf16[512,256]{0,1:T(8,128)(2,1)S(1)}, bf16[512,256]{0,1:T(8,128)(2,1)S(1)}, u32[]{:S(2)}, u32[]{:S(2)}) %collective-permute-start) | collective-permute-done | bytes 262176 | tf_op jit(solution)/shard_map/ppermute | solution.py:30
  18.6 3.9 %collective-permute-done.1 = bf16[512,256]{0,1:T(8,128)(2,1)S(1)} collective-permute-done((bf16[512,256]{0,1:T(8,128)(2,1)S(1)}, bf16[512,256]{0,1:T(8,128)(2,1)S(1)}, u32[]{:S(2)}, u32[]{:S(2)}) %collective-permute-start.1) | collective-permute-done | bytes 262176 | tf_op jit(solution)/shard_map/ppermute | solution.py:30
  22.9 5.4 %collective-permute-done.2 = bf16[512,256]{0,1:T(8,128)(2,1)S(1)} collective-permute-done((bf16[512,256]{0,1:T(8,128)(2,1)S(1)}, bf16[512,256]{0,1:T(8,128)(2,1)S(1)}, u32[]{:S(2)}, u32[]{:S(2)}) %collective-permute-start.2) | collective-permute-done | bytes 262176 | tf_op jit(solution)/shard_map/ppermute | solution.py:30
  28.6 12.2 %all-gather.5.cloned.1.call-done = bf16[512,1024]{0,1:T(8,128)(2,1)} async-done(((bf16[512,256]{0,1:T(8,128)(2,1)}), bf16[512,1024]{0,1:T(8,128)(2,1)}) %all-gather.5.cloned.1.call-update) | async-done | bytes 1048592 | tf_op jit(solution)/shard_map/all_gather | solution.py:35
  40.8 17.3 %while.57 = (s32[]{:T(128)}, f32[16,512]{1,0:T(8,128)S(1)}, f32[16,512]{1,0:T(8,128)S(1)}, pred[1,4]{1,0:T(4,128)(4,1)S(1)}, bf16[512,1024]{0,1:T(8,128)(2,1)}, ...) while((s32[]{:T(128)}, f32[16,512]{1,0:T(8,128)S(1)}, ...), condition=%wide.region_7.8_spmd.clone, body=%wide.region_2.7_spmd.clone.sunk | while | flops 142622736 | bytes 10658168 | solution.py:88
  58.1 11.6 %pmax.7 = bf16[16,512]{1,0:T(8,128)(2,1)S(1)} all-reduce(bf16[16,512]{1,0:T(8,128)(2,1)S(1)} %convert_element_type.89), channel_id=1, replica_groups=mesh['groups'=2,'row'=4,'col'=4] {'col'}, use_global_device_ids=true, to_apply=%region_8.9 | all-reduce | flops 8192 | bytes 32768 | tf_op jit(solution)/shard_map/pmax | solution.py:89
  69.7 10.3 %psum.7 = f32[16,512]{1,0:T(8,128)S(1)} all-reduce(f32[16,512]{1,0:T(8,128)S(1)} %exponential_multiply_fusion), channel_id=1, replica_groups=mesh['groups'=2,'row'=4,'col'=4] {'col'}, use_global_device_ids=true, to_apply=%region_9.10 | all-reduce | flops 8192 | bytes 65536 | tf_op jit(solution)/shard_map/psum | solution.py:90
  80.3 36.9 %while.58 = (s32[]{:T(128)}, f32[512,1024]{0,1:T(8,128)S(1)}, pred[1,4]{1,0:T(4,128)(4,1)S(1)}, bf16[512,1024]{0,1:T(8,128)(2,1)}, bf16[512,1024]{0,1:T(8,128)(2...) while((s32[]{:T(128)}, f32[512,1024]{0,1:T(8,128)S(1)}, ...), condition=%wide.region_13.14_spmd.clone, body=%wide.region_10.13_spmd.clone.sunk | while | flops 275251200 | bytes 11083640 | solution.py:115
  81.0 8.6 %conditional.10 = (f32[512,1024]{0,1:T(8,128)S(1)}) conditional(s32[]{:T(128)} %bitcast.69, f32[512,1024]{0,1:T(8,128)S(1)} %get-tuple-element.1617, (pred[4,4]{1,0:T(4,128)(4,1)S(1)}, s32[]{:T(128)}, s32[]{:T(128)}, bf16[512,1024]{0,1:T(8,128)(2,1)}, bf16[512,1024]{0,1:T(8,128)(2,1)S(1)}, /*index=5*/f32[16,512]{1,0:T(8,128)S(1)}, ...), branch_computations={%region_11.11_spmd, %region_12.12_spmd} | conditional | flops 275251200 | bytes 11083342 | solution.py:113
  90.2 8.6 %conditional.10 = (f32[512,1024]{0,1:T(8,128)S(1)}) conditional(s32[]{:T(128)} %bitcast.69, f32[512,1024]{0,1:T(8,128)S(1)} %get-tuple-element.1617, (pred[4,4]{1,0:T(4,128)(4,1)S(1)}, s32[]{:T(128)}, s32[]{:T(128)}, bf16[512,1024]{0,1:T(8,128)(2,1)}, bf16[512,1024]{0,1:T(8,128)(2,1)S(1)}, /*index=5*/f32[16,512]{1,0:T(8,128)S(1)}, ...), branch_computations={%region_11.11_spmd, %region_12.12_spmd} | conditional | flops 275251200 | bytes 11083342 | solution.py:113
  92.8 3.8 %fusion.9 = f32[16,512,64]{1,2,0:T(8,128)} fusion(bf16[128,16,64]{0,2,1:T(8,128)(2,1)S(1)} %bitcast.81, bf16[128,16,64]{0,2,1:T(8,128)(2,1)} %bitcast.82, bf16[512,16,64]{0,2,1:T(8,128)(2,1)S(1)} %bitcast.72, f32[16,512]{1,0:T(8,128)S(1)} %get-tuple-element.1154, f32[16,512]{1,0:T(8,128)S(1)} %get-tuple-element.1153, ...), kind=kOutput, calls=%fused_computation.15 | convolution fusion | flops 274726912 | bytes 3736064 | tf_op jit(solution)/shard_map/while/body/eval_jaxpr/cond/branch_1_fun/hqk,khd->qhd/dot_general | solution.py:105
  99.4 8.6 %conditional.10 = (f32[512,1024]{0,1:T(8,128)S(1)}) conditional(s32[]{:T(128)} %bitcast.69, f32[512,1024]{0,1:T(8,128)S(1)} %get-tuple-element.1617, (pred[4,4]{1,0:T(4,128)(4,1)S(1)}, s32[]{:T(128)}, s32[]{:T(128)}, bf16[512,1024]{0,1:T(8,128)(2,1)}, bf16[512,1024]{0,1:T(8,128)(2,1)S(1)}, /*index=5*/f32[16,512]{1,0:T(8,128)S(1)}, ...), branch_computations={%region_11.11_spmd, %region_12.12_spmd} | conditional | flops 275251200 | bytes 11083342 | solution.py:113
  108.6 8.6 %conditional.10 = (f32[512,1024]{0,1:T(8,128)S(1)}) conditional(s32[]{:T(128)} %bitcast.69, f32[512,1024]{0,1:T(8,128)S(1)} %get-tuple-element.1617, (pred[4,4]{1,0:T(4,128)(4,1)S(1)}, s32[]{:T(128)}, s32[]{:T(128)}, bf16[512,1024]{0,1:T(8,128)(2,1)}, bf16[512,1024]{0,1:T(8,128)(2,1)S(1)}, /*index=5*/f32[16,512]{1,0:T(8,128)S(1)}, ...), branch_computations={%region_11.11_spmd, %region_12.12_spmd} | conditional | flops 275251200 | bytes 11083342 | solution.py:113
  119.5 29.6 %reduce-scatter.5.cloned.1.call-done = f32[512,256]{0,1:T(8,128)} async-done(((f32[512,1024]{0,1:T(8,128)}), f32[512,256]{0,1:T(8,128)}) %reduce-scatter.5.cloned.1.call-update) | async-done | bytes 524304 | tf_op jit(solution)/shard_map/reduce_scatter | solution.py:116
  151.0 17.0 %all-gather.9.cloned.1.call-done = bf16[512,1024]{0,1:T(8,128)(2,1)} async-done(((bf16[512,256]{0,1:T(8,128)(2,1)}), bf16[512,1024]{0,1:T(8,128)(2,1)}) %all-gather.9.cloned.1.call-update) | async-done | bytes 1048592 | tf_op jit(solution)/shard_map/all_gather | solution.py:120
  168.0 18.8 %all-gather.11.cloned.1.call-done = bf16[512,1024]{0,1:T(8,128)(2,1)} async-done(((bf16[512,256]{0,1:T(8,128)(2,1)}), bf16[512,1024]{0,1:T(8,128)(2,1)}) %all-gather.11.cloned.1.call-update) | async-done | bytes 1048592 | tf_op jit(solution)/shard_map/all_gather | solution.py:121
  193.5 51.9 %while.59 = (s32[]{:T(128)}, f32[512,1024]{0,1:T(8,128)}, f32[512,1024]{0,1:T(8,128)}, f32[512,1024]{0,1:T(8,128)}, pred[1,4]{1,0:T(4,128)(4,1)S(1)}, /*index=5*...) while((s32[]{:T(128)}, f32[512,1024]{0,1:T(8,128)}, ...), condition=%wide.region_18.19_spmd.clone, body=%wide.region_15.18_spmd.clone.sunk | while | flops 683016192 | bytes 48078884 | solution.py:180
  194.1 12.3 %conditional.11 = ((f32[512,1024]{0,1:T(8,128)}, f32[512,1024]{0,1:T(8,128)}, f32[512,1024]{0,1:T(8,128)})) conditional(s32[]{:T(128)} %bitcast.70, (f32[512,1024]{0,1:T(8,128)}, f32[512,1024]{0,1:T(8,128)}, f32[512,1024]{0,1:T(8,128)}) %tuple.199, (pred[4,4]{1,0:T(4,128)(4,1)S(1)}, s32[]{:T(128)}, s32[]{:T(128)}, bf16[512,1024]{0,1:T(8,128)(2,1)}, ...), branch_computations={%region_16.16_spmd, %region_17.17_spmd} | conditional | flops 683016192 | bytes 48078500 | solution.py:173
  207.0 12.3 %conditional.11 = ((f32[512,1024]{0,1:T(8,128)}, f32[512,1024]{0,1:T(8,128)}, f32[512,1024]{0,1:T(8,128)})) conditional(s32[]{:T(128)} %bitcast.70, (f32[512,1024]{0,1:T(8,128)}, f32[512,1024]{0,1:T(8,128)}, f32[512,1024]{0,1:T(8,128)}) %tuple.199, (pred[4,4]{1,0:T(4,128)(4,1)S(1)}, s32[]{:T(128)}, s32[]{:T(128)}, bf16[512,1024]{0,1:T(8,128)(2,1)}, ...), branch_computations={%region_16.16_spmd, %region_17.17_spmd} | conditional | flops 683016192 | bytes 48078500 | solution.py:173
  220.0 12.3 %conditional.11 = ((f32[512,1024]{0,1:T(8,128)}, f32[512,1024]{0,1:T(8,128)}, f32[512,1024]{0,1:T(8,128)})) conditional(s32[]{:T(128)} %bitcast.70, (f32[512,1024]{0,1:T(8,128)}, f32[512,1024]{0,1:T(8,128)}, f32[512,1024]{0,1:T(8,128)}) %tuple.199, (pred[4,4]{1,0:T(4,128)(4,1)S(1)}, s32[]{:T(128)}, s32[]{:T(128)}, bf16[512,1024]{0,1:T(8,128)(2,1)}, ...), branch_computations={%region_16.16_spmd, %region_17.17_spmd} | conditional | flops 683016192 | bytes 48078500 | solution.py:173
  233.0 12.3 %conditional.11 = ((f32[512,1024]{0,1:T(8,128)}, f32[512,1024]{0,1:T(8,128)}, f32[512,1024]{0,1:T(8,128)})) conditional(s32[]{:T(128)} %bitcast.70, (f32[512,1024]{0,1:T(8,128)}, f32[512,1024]{0,1:T(8,128)}, f32[512,1024]{0,1:T(8,128)}) %tuple.199, (pred[4,4]{1,0:T(4,128)(4,1)S(1)}, s32[]{:T(128)}, s32[]{:T(128)}, bf16[512,1024]{0,1:T(8,128)(2,1)}, ...), branch_computations={%region_16.16_spmd, %region_17.17_spmd} | conditional | flops 683016192 | bytes 48078500 | solution.py:173
  256.9 35.4 %reduce-scatter.11.cloned.1.call-done = f32[512,256]{1,0:T(8,128)} async-done(((f32[512,1024]{1,0:T(8,128)}), f32[512,256]{1,0:T(8,128)}) %reduce-scatter.11.cloned.1.call-update) | async-done | bytes 524304 | tf_op jit(solution)/shard_map/reduce_scatter | solution.py:186
  294.1 31.5 %reduce-scatter.7.cloned.1.call-done = f32[512,256]{1,0:T(8,128)} async-done(((f32[512,1024]{1,0:T(8,128)}), f32[512,256]{1,0:T(8,128)}) %reduce-scatter.7.cloned.1.call-update) | async-done | bytes 524304 | tf_op jit(solution)/shard_map/reduce_scatter | solution.py:181
  327.4 44.5 %reduce-scatter.9.cloned.1.call-done = f32[512,256]{1,0:T(8,128)} async-done(((f32[512,1024]{1,0:T(8,128)}), f32[512,256]{1,0:T(8,128)}) %reduce-scatter.9.cloned.1.call-update) | async-done | bytes 524304 | tf_op jit(solution)/shard_map/reduce_scatter | solution.py:185
  (210 shorter events, 142.1 us)
Async XLA Ops:
  7.2 15.3 %copy-start.9 = (s32[4]{0:T(128)S(1)}, s32[4]{0:T(128)}, u32[]{:S(2)}) copy-start(s32[4]{0:T(128)} %param.23) | copy-start | bytes 52
  7.2 15.4 %copy-start.8 = (s32[4,16]{1,0:T(4,128)S(1)}, s32[4,16]{1,0:T(4,128)}, u32[]{:S(2)}) copy-start(s32[4,16]{1,0:T(4,128)} %param.22) | copy-start | bytes 772
  7.2 33.6 %all-gather.5.cloned.1.call-start = ((), (), s32[]{:S(2)}) async-start(), calls=%async_computation.4 | async-start | bytes 1310720 | tf_op jit(solution)/shard_map/all_gather | solution.py:35
  9.1 71.0 %all-gather.7.cloned.1.call-start = ((), (), s32[]{:S(2)}) async-start(), calls=%async_computation.5 | async-start | bytes 1310720 | tf_op jit(solution)/shard_map/all_gather | solution.py:36
  10.2 6.5 %collective-permute-start = (bf16[512,256]{0,1:T(8,128)(2,1)S(1)}, bf16[512,256]{0,1:T(8,128)(2,1)S(1)}, u32[]{:S(2)}, u32[]{:S(2)}) collective-permute-start(bf16[512,256]{0,1:T(8,128)(2,1)S(1)} %copy.35), channel_id=1, source_target_pairs={{0,1},{1,2},{2,3},{3,0},{4,5},{5,6},{6,7},{7,4},{8,9},{9,10},{10,1... | collective-permute-start | bytes 786440 | tf_op jit(solution)/shard_map/ppermute | solution.py:30
  16.7 5.8 %collective-permute-start.1 = (bf16[512,256]{0,1:T(8,128)(2,1)S(1)}, bf16[512,256]{0,1:T(8,128)(2,1)S(1)}, u32[]{:S(2)}, u32[]{:S(2)}) collective-permute-start(bf16[512,256]{0,1:T(8,128)(2,1)S(1)} %collective-permute-done), channel_id=1, source_target_pairs={{0,1},{1,2},{2,3},{3,0},{4,5},{5,6},{6,7},{7,4},{8,9},{9,10},{10,1... | collective-permute-start | bytes 786440 | tf_op jit(solution)/shard_map/ppermute | solution.py:30
  18.5 130.6 %reduce-scatter.5.cloned.1.call-start = ((), (), s32[]{:S(2)}) async-start(), calls=%async_computation.6 | async-start | bytes 2621440 | tf_op jit(solution)/shard_map/reduce_scatter | solution.py:116
  22.5 5.8 %collective-permute-start.2 = (bf16[512,256]{0,1:T(8,128)(2,1)S(1)}, bf16[512,256]{0,1:T(8,128)(2,1)S(1)}, u32[]{:S(2)}, u32[]{:S(2)}) collective-permute-start(bf16[512,256]{0,1:T(8,128)(2,1)S(1)} %collective-permute-done.1), channel_id=1, source_target_pairs={{0,1},{1,2},{2,3},{3,0},{4,5},{5,6},{6,7},{7,4},{8,9},{9,10},{10,1... | collective-permute-start | bytes 786440 | tf_op jit(solution)/shard_map/ppermute | solution.py:30
  117.2 1.4 copy-start.7
  118.6 49.4 %all-gather.9.cloned.1.call-start = ((), (), s32[]{:S(2)}) async-start(), calls=%async_computation.7 | async-start | bytes 1310720 | tf_op jit(solution)/shard_map/all_gather | solution.py:120
  119.5 67.3 %all-gather.11.cloned.1.call-start = ((), (), s32[]{:S(2)}) async-start(), calls=%async_computation.8 | async-start | bytes 1310720 | tf_op jit(solution)/shard_map/all_gather | solution.py:121
  150.9 141.4 %reduce-scatter.11.cloned.1.call-start = ((), (), s32[]{:S(2)}) async-start(), calls=%async_computation.11 | async-start | bytes 2621440 | tf_op jit(solution)/shard_map/reduce_scatter | solution.py:186
  190.3 3.2 copy-start
  200.6 1.6 copy-start.1
  202.7 1.3 copy-start.2
  213.6 1.6 copy-start.1
  215.7 1.3 copy-start.2
  226.5 1.6 copy-start.1
  228.7 1.3 copy-start.2
  239.5 1.6 copy-start.1
  248.2 1.6 copy-start.3
  248.3 77.3 %reduce-scatter.7.cloned.1.call-start = ((), (), s32[]{:S(2)}) async-start(), calls=%async_computation.9 | async-start | bytes 2621440 | tf_op jit(solution)/shard_map/reduce_scatter | solution.py:181
  251.7 1.6 copy-start.5
  251.7 120.2 %reduce-scatter.9.cloned.1.call-start = ((), (), s32[]{:S(2)}) async-start(), calls=%async_computation.10 | async-start | bytes 2621440 | tf_op jit(solution)/shard_map/reduce_scatter | solution.py:185
  (3 other events, 3.6 us)
Sparse Core Ops, SparseCore 0:
  10.2 30.6 all-gather.4
  43.0 27.4 all-gather.6
  118.7 30.4 reduce-scatter.4
  151.2 16.7 all-gather.8
  170.0 16.7 all-gather.10
  248.4 43.8 reduce-scatter.10
  294.8 30.7 reduce-scatter.6
  328.0 43.8 reduce-scatter.8
